TPU v7x, 256 devices: a whole 4x4x8 slice. The times are simulated.
256 devices in a mesh: dp: 4 (over y), sx: 4 (over x_lo, core), sy: 16 (over z, x_hi).
Axes of the slice: x: 4 (x_hi: 2, x_lo: 2; x = x_hi * 2 + x_lo), y: 4, z: 8, core: 2. Of those that a mesh axis runs over, the one named last changes fastest.
Arguments:
- features: bfloat16 [4, 4, 16, 3072, 128], P('dp', 'sx', 'sy'), may hold values from -6 to 6
- cotangent: bfloat16 [4, 4, 16, 3072, 128], P('dp', 'sx', 'sy'), may hold values from -6 to 6
- weights: bfloat16 [27, 128, 128], replicated, may hold values from -0.109375 to 0.109375
- tables: int32 [4, 4, 16, 27, 24], P('dp', 'sx', 'sy'), may hold values from 0 to 56, as said below
- send_lists: int32 [4, 4, 16, 4], P('dp', 'sx', 'sy'), may hold values from 0 to 23, as said below
- counts: int32 [4, 4, 16], P('dp', 'sx', 'sy'), may hold values from 6 to 24, as said below
Outputs:
- output: bfloat16 [4, 4, 16, 3072, 128], P('dp', 'sx', 'sy')
- input_grad: bfloat16 [4, 4, 16, 3072, 128], P('dp', 'sx', 'sy')
- weight_grad: float32 [27, 128, 128], replicated
Inputs may be any that keep to these rules, and one draw needn't show every extreme that they name: `tables`: entries below 24 name a block of the tile, 24 + n * 4 + s' the s'-th sent block of neighbour direction n, 56 the empty block; under offset 27 // 2 every block reads itself. `send_lists`: the 4 blocks of one tile are distinct. `counts`: some tile has all 24 blocks active.
All inputs are finite; a program needn't handle non-finite values.
Results may differ from a plain program's by a relative error of at most 0.001.
Values may be sent and summed in bfloat16 or wider, within the bound.
A program may use at most 64 MiB of HBM per device.

v0:
```python
import math
import jax
import jax.numpy as jnp
from jax import lax
from jax.sharding import PartitionSpec as P

directions = ((-1, -1), (-1, 0), (-1, 1), (0, -1), (0, 1), (1, -1), (1, 0), (1, 1))


def shifted(block, axis, distance):
    devices = range(lax.axis_size(axis))
    route = [(i - distance, i) for i in devices if i - distance in devices]
    return lax.ppermute(block, axis, route)


def padded(cells, sides, width):
    for axis, dim in sides:
        count = lax.axis_size(axis)
        ends = count - 1
        head = lax.slice_in_dim(cells, 0, width, axis=dim)
        tail = lax.slice_in_dim(cells, cells.shape[dim] - width, cells.shape[dim], axis=dim)
        cells = jnp.concatenate(
            [
                lax.ppermute(tail, axis, [(i, (i + 1) % count) for i in range(ends)]),
                cells,
                lax.ppermute(head, axis, [((i + 1) % count, i) for i in range(ends)]),
            ],
            axis=dim,
        )
    return cells


def local(features, cotangent, weights, tables, send_lists, counts):
    num_blocks = tables.shape[4]
    num_sent = send_lists.shape[3]
    offsets = weights.shape[0]
    channels = weights.shape[1]
    width_block = features.shape[3] // num_blocks
    group_size = 4
    active = (jnp.arange(num_blocks) < counts.reshape(())).astype(jnp.bfloat16)[:, None, None]
    active_full = active.astype(jnp.float32)
    blocks_in = features.reshape(num_blocks, width_block, channels) * active
    blocks_grad = cotangent.reshape(num_blocks, width_block, channels) * active
    offset_table = tables.reshape(offsets, num_blocks)
    sent_ids = send_lists.reshape(num_sent)
    groups = jnp.arange(num_blocks // group_size)

    def grad_group(accum, group):
        start = group * group_size
        picks = lax.dynamic_slice_in_dim(offset_table, start, group_size, 1)
        grad_rows = lax.dynamic_slice_in_dim(blocks_grad, start, group_size, 0)
        contrib = jnp.einsum(
            "gvd,kcd->kgvc", grad_rows, weights, preferred_element_type=jnp.float32
        )
        accum = accum.at[picks.reshape(-1)].add(
            contrib.reshape(offsets * group_size, width_block, channels)
        )
        return (accum, None)

    num_ext = num_blocks + 8 * num_sent + 1
    grad_ext, unused_rows = lax.scan(
        grad_group, jnp.zeros((num_ext, width_block, channels), jnp.float32), groups
    )
    halo_grads = grad_ext[num_blocks : num_blocks + 8 * num_sent].reshape(
        8, num_sent * width_block, channels
    )
    received = jnp.zeros((num_sent * width_block, channels), jnp.float32)
    for slot_index, (step_x, step_y) in enumerate(directions):
        portion = halo_grads[slot_index]
        if step_x != 0:
            portion = shifted(portion, "sx", step_x)
        if step_y != 0:
            portion = shifted(portion, "sy", step_y)
        received = received + portion
    local_grad = (
        grad_ext[:num_blocks].at[sent_ids].add(received.reshape(num_sent, width_block, channels))
    )
    input_grad = (local_grad * active_full).astype(jnp.bfloat16).reshape(features.shape)
    outgoing = blocks_in[sent_ids].reshape(1, 1, num_sent * width_block, channels)
    bordered = padded(outgoing, (("sx", 0), ("sy", 1)), 1)
    neighbours = [
        bordered[1 + step_x, 1 + step_y].reshape(num_sent, width_block, channels)
        for step_x, step_y in directions
    ]
    extended = jnp.concatenate(
        [blocks_in] + neighbours + [jnp.zeros((1, width_block, channels), jnp.bfloat16)], axis=0
    )

    def forward_group(accum, group):
        start = group * group_size
        picks = lax.dynamic_slice_in_dim(offset_table, start, group_size, 1)
        gathered = extended[picks]
        grad_rows = lax.dynamic_slice_in_dim(blocks_grad, start, group_size, 0)
        rows_active = lax.dynamic_slice_in_dim(active_full, start, group_size, 0)
        outputs = jnp.einsum("kgvc,kcd->gvd", gathered, weights, preferred_element_type=jnp.float32)
        accum = accum + jnp.einsum(
            "kgvc,gvd->kcd", gathered, grad_rows, preferred_element_type=jnp.float32
        )
        return (accum, (outputs * rows_active).astype(jnp.bfloat16))

    weight_part, outputs = lax.scan(
        forward_group, jnp.zeros((offsets, channels, channels), jnp.float32), groups
    )
    output = outputs.reshape(features.shape)
    total = (
        num_blocks * width_block * lax.axis_size("dp") * lax.axis_size("sx") * lax.axis_size("sy")
    )
    scaled_part = weight_part * (1.0 / math.sqrt(total))
    weight_grad = lax.psum(scaled_part, ("dp", "sx", "sy"))
    return (output, input_grad, weight_grad)


def solution(mesh):
    return jax.shard_map(
        local,
        mesh=mesh,
        in_specs=(
            P("dp", "sx", "sy", None, None),
            P("dp", "sx", "sy", None, None),
            P(),
            P("dp", "sx", "sy", None, None),
            P("dp", "sx", "sy", None),
            P("dp", "sx", "sy"),
        ),
        out_specs=(P("dp", "sx", "sy", None, None), P("dp", "sx", "sy", None, None), P()),
        check_vma=False,
    )
```

profile of v0, /device:TPU:2, one launch (start us, length us, event | category | flops | bytes accessed | tf_op | source)
XLA Modules:
  0.0 617.5 jit_solution(9292657915912878841)
XLA Ops:
  8.5 3.2 constant_dynamic-update-slice_fusion.9
  14.3 2.4 collective-permute-start
  19.8 184.4 %while.23 = (s32[]{:T(128)}, f32[57,128,128]{2,1,0:T(8,128)}, s32[6]{0:T(128)S(1)}, s32[27,24]{1,0:T(8,128)}, bf16[24,128,128]{2,1,0:T(8,128)(2,1)}, /*index=5*/...) while((s32[]{:T(128)}, f32[57,128,128]{2,1,0:T(8,128)}, s32[6]{0:T(128)S(1)}, ...), condition=%wide.region_4.5_spmd, body=%wide.region_2.0_spmd.sunk | while | flops 454754624 | bytes 43486336 | solution.py:61
  24.3 3.3 copy.22
  27.6 22.9 %scatter_fusion = f32[57,128,128]{2,1,0:T(8,128)} fusion(f32[57,128,128]{2,1,0:T(8,128)} %get-tuple-element.307, s32[108]{0:T(128)S(1)} %fusion.33, f32[108,128,128]{2,1,0:T(8,128)} %bitcast.107), kind=kCustom, calls=%fused_computation.2.clone.1 | custom fusion | flops 1769472 | bytes 21234096 | tf_op jit(solution)/shard_map/while/body/eval_jaxpr/scatter-add | solution.py:55
  55.0 3.3 copy.22
  58.3 22.9 %scatter_fusion = f32[57,128,128]{2,1,0:T(8,128)} fusion(f32[57,128,128]{2,1,0:T(8,128)} %get-tuple-element.307, s32[108]{0:T(128)S(1)} %fusion.33, f32[108,128,128]{2,1,0:T(8,128)} %bitcast.107), kind=kCustom, calls=%fused_computation.2.clone.1 | custom fusion | flops 1769472 | bytes 21234096 | tf_op jit(solution)/shard_map/while/body/eval_jaxpr/scatter-add | solution.py:55
  85.7 3.3 copy.22
  89.1 22.8 %scatter_fusion = f32[57,128,128]{2,1,0:T(8,128)} fusion(f32[57,128,128]{2,1,0:T(8,128)} %get-tuple-element.307, s32[108]{0:T(128)S(1)} %fusion.33, f32[108,128,128]{2,1,0:T(8,128)} %bitcast.107), kind=kCustom, calls=%fused_computation.2.clone.1 | custom fusion | flops 1769472 | bytes 21234096 | tf_op jit(solution)/shard_map/while/body/eval_jaxpr/scatter-add | solution.py:55
  116.4 3.3 copy.22
  119.7 23.0 %scatter_fusion = f32[57,128,128]{2,1,0:T(8,128)} fusion(f32[57,128,128]{2,1,0:T(8,128)} %get-tuple-element.307, s32[108]{0:T(128)S(1)} %fusion.33, f32[108,128,128]{2,1,0:T(8,128)} %bitcast.107), kind=kCustom, calls=%fused_computation.2.clone.1 | custom fusion | flops 1769472 | bytes 21234096 | tf_op jit(solution)/shard_map/while/body/eval_jaxpr/scatter-add | solution.py:55
  147.2 3.3 copy.22
  150.6 22.9 %scatter_fusion = f32[57,128,128]{2,1,0:T(8,128)} fusion(f32[57,128,128]{2,1,0:T(8,128)} %get-tuple-element.307, s32[108]{0:T(128)S(1)} %fusion.33, f32[108,128,128]{2,1,0:T(8,128)} %bitcast.107), kind=kCustom, calls=%fused_computation.2.clone.1 | custom fusion | flops 1769472 | bytes 21234096 | tf_op jit(solution)/shard_map/while/body/eval_jaxpr/scatter-add | solution.py:55
  177.9 3.3 copy.22
  181.3 22.9 %scatter_fusion = f32[57,128,128]{2,1,0:T(8,128)} fusion(f32[57,128,128]{2,1,0:T(8,128)} %get-tuple-element.307, s32[108]{0:T(128)S(1)} %fusion.33, f32[108,128,128]{2,1,0:T(8,128)} %bitcast.107), kind=kCustom, calls=%fused_computation.2.clone.1 | custom fusion | flops 1769472 | bytes 21234096 | tf_op jit(solution)/shard_map/while/body/eval_jaxpr/scatter-add | solution.py:55
  204.3 4.3 collective-permute-start.2
  208.6 2.9 fusion.17
  213.4 3.6 collective-permute-start.6
  223.6 10.0 %collective-permute-done.3 = bf16[3,1,512,128]{3,2,1,0:T(8,128)(2,1)S(1)} collective-permute-done((bf16[3,1,512,128]{3,2,1,0:T(8,128)(2,1)S(1)}, bf16[3,1,512,128]{3,2,1,0:T(8,128)(2,1)S(1)}, u32[]{:S(2)}, u32[]{:S(2)}) %collective-permute-start.3) | collective-permute-done | bytes 393248 | tf_op jit(solution)/shard_map/ppermute | solution.py:26
  233.5 6.1 collective-permute-start.10
  244.8 79.9 %while.24 = (s32[]{:T(128)}, f32[27,128,128]{2,1,0:T(8,128)}, bf16[6,4,128,128]{3,2,1,0:T(8,128)(2,1)}, s32[6]{0:T(128)}, s32[27,24]{1,0:T(8,128)}, /*index=5*/b...) while((s32[]{:T(128)}, f32[27,128,128]{2,1,0:T(8,128)}, ...), condition=%wide.region_1.0_spmd.clone, body=%wide.region_0.1_spmd.clone.sunk | while | flops 906986816 | bytes 33004880 | solution.py:101
  248.2 2.7 gather_fusion
  251.0 3.0 fusion.39
  254.0 2.9 bitcast_add_fusion.2
  261.5 2.7 gather_fusion
  264.3 3.0 fusion.39
  267.3 2.9 bitcast_add_fusion.2
  274.8 2.7 gather_fusion
  277.6 3.0 fusion.39
  280.6 2.9 bitcast_add_fusion.2
  288.1 2.7 gather_fusion
  290.9 3.0 fusion.39
  294.0 2.9 bitcast_add_fusion.2
  301.5 2.7 gather_fusion
  304.2 3.0 fusion.39
  307.3 2.9 bitcast_add_fusion.2
  314.8 2.7 gather_fusion
  317.5 3.0 fusion.39
  320.6 2.9 bitcast_add_fusion.2
  324.7 4.2 collective-permute-start.7
  328.9 4.3 collective-permute-start.4
  333.2 3.0 broadcast_multiply_fusion
  337.5 6.1 collective-permute-start.15
  344.9 6.1 collective-permute-start.8
  353.8 9.3 %collective-permute-done.15 = f32[512,128]{1,0:T(8,128)S(1)} collective-permute-done((f32[512,128]{1,0:T(8,128)}, f32[512,128]{1,0:T(8,128)S(1)}, u32[]{:S(2)}, u32[]{:S(2)}) %collective-permute-start.15) | collective-permute-done | bytes 262176 | tf_op jit(solution)/shard_map/ppermute | solution.py:13
  363.1 5.7 collective-permute-done.8
  371.9 235.9 %all-reduce.2.cloned.1.call-done = f32[27,128,128]{2,1,0:T(8,128)} async-done(((f32[27,128,128]{2,1,0:T(8,128)}), f32[27,128,128]{2,1,0:T(8,128)}) %all-reduce.2.cloned.1.call-update) | async-done | bytes 1769488 | tf_op jit(solution)/shard_map/psum | solution.py:109
  607.8 2.9 copy.52
  (138 shorter events, 75.1 us)
Async XLA Ops:
  7.2 600.6 %all-reduce.2.cloned.1.call-start = ((), (), s32[]{:S(2)}) async-start(), calls=%async_computation | async-start | bytes 3538944 | tf_op jit(solution)/shard_map/psum | solution.py:109
  8.5 8.2 %copy-start.3 = (s32[1,1,1,27,24]{3,4,2,1,0:T(8,128)S(1)}, s32[1,1,1,27,24]{3,4,2,1,0:T(8,128)}, u32[]{:S(2)}) copy-start(s32[1,1,1,27,24]{3,4,2,1,0:T(8,128)} %param.13) | copy-start | bytes 7780
  12.3 191.9 %collective-permute-start.1 = (bf16[1,1,512,128]{3,2,1,0:T(8,128)(2,1)S(1)}, bf16[1,1,512,128]{3,2,1,0:T(8,128)(2,1)S(1)}, u32[]{:S(2)}, u32[]{:S(2)}) collective-permute-start(bf16[1,1,512,128]{3,2,1,0:T(8,128)(2,1)S(1)} %bitcast.116), channel_id=1, source_target_pairs={{16,0},{32,16},{48,32},{17,1},{33,17},{49,33},{18,2},{34,18},{50,3... | collective-permute-start | bytes 393224 | tf_op jit(solution)/shard_map/ppermute | solution.py:26
  14.3 189.9 %collective-permute-start = (bf16[1,1,512,128]{3,2,1,0:T(8,128)(2,1)S(1)}, bf16[1,1,512,128]{3,2,1,0:T(8,128)(2,1)S(1)}, u32[]{:S(2)}, u32[]{:S(2)}) collective-permute-start(bf16[1,1,512,128]{3,2,1,0:T(8,128)(2,1)S(1)} %bitcast.117), channel_id=1, source_target_pairs={{0,16},{16,32},{32,48},{1,17},{17,33},{33,49},{2,18},{18,34},{34,5... | collective-permute-start | bytes 393224 | tf_op jit(solution)/shard_map/ppermute | solution.py:24
  204.3 16.7 %collective-permute-start.2 = (bf16[3,1,512,128]{3,2,1,0:T(8,128)(2,1)S(1)}, bf16[3,1,512,128]{3,2,1,0:T(8,128)(2,1)S(1)}, u32[]{:S(2)}, u32[]{:S(2)}) collective-permute-start(bf16[3,1,512,128]{3,2,1,0:T(8,128)(2,1)S(1)} %pad_maximum_fusion), channel_id=1, source_target_pairs={{0,1},{1,2},{2,3},{3,4},{4,5},{5,6},{6,7},{7,8},{8,9},{9,10},{10,1... | collective-permute-start | bytes 1179656 | tf_op jit(solution)/shard_map/ppermute | solution.py:24
  211.4 113.2 %collective-permute-start.14 = (f32[512,128]{1,0:T(8,128)}, f32[512,128]{1,0:T(8,128)}, u32[]{:S(2)}, u32[]{:S(2)}) collective-permute-start(f32[512,128]{1,0:T(8,128)} %bitcast.30), channel_id=1, source_target_pairs={{0,16},{16,32},{32,48},{1,17},{17,33},{33,49},{2,18},{18,34},{34,5... | collective-permute-start | bytes 786440 | tf_op jit(solution)/shard_map/ppermute | solution.py:13
  213.4 115.5 %collective-permute-start.6 = (f32[512,128]{1,0:T(8,128)}, f32[512,128]{1,0:T(8,128)}, u32[]{:S(2)}, u32[]{:S(2)}) collective-permute-start(f32[512,128]{1,0:T(8,128)} %bitcast.24), channel_id=1, source_target_pairs={{16,0},{32,16},{48,32},{17,1},{33,17},{49,33},{18,2},{34,18},{50,3... | collective-permute-start | bytes 786440 | tf_op jit(solution)/shard_map/ppermute | solution.py:13
  217.0 119.1 %collective-permute-start.13 = (f32[512,128]{1,0:T(8,128)}, f32[512,128]{1,0:T(8,128)}, u32[]{:S(2)}, u32[]{:S(2)}) collective-permute-start(f32[512,128]{1,0:T(8,128)} %bitcast.29), channel_id=1, source_target_pairs={{0,16},{16,32},{32,48},{1,17},{17,33},{33,49},{2,18},{18,34},{34,5... | collective-permute-start | bytes 786440 | tf_op jit(solution)/shard_map/ppermute | solution.py:13
  218.9 118.5 %collective-permute-start.11 = (f32[512,128]{1,0:T(8,128)}, f32[512,128]{1,0:T(8,128)}, u32[]{:S(2)}, u32[]{:S(2)}) collective-permute-start(f32[512,128]{1,0:T(8,128)} %bitcast.28), channel_id=1, source_target_pairs={{0,16},{16,32},{32,48},{1,17},{17,33},{33,49},{2,18},{18,34},{34,5... | collective-permute-start | bytes 786440 | tf_op jit(solution)/shard_map/ppermute | solution.py:13
  220.9 12.6 %collective-permute-start.3 = (bf16[3,1,512,128]{3,2,1,0:T(8,128)(2,1)S(1)}, bf16[3,1,512,128]{3,2,1,0:T(8,128)(2,1)S(1)}, u32[]{:S(2)}, u32[]{:S(2)}) collective-permute-start(bf16[3,1,512,128]{3,2,1,0:T(8,128)(2,1)S(1)} %pad_maximum_fusion), channel_id=1, source_target_pairs={{1,0},{2,1},{3,2},{4,3},{5,4},{6,5},{7,6},{8,7},{9,8},{10,9},{11,1... | collective-permute-start | bytes 1179656 | tf_op jit(solution)/shard_map/ppermute | solution.py:26
  233.5 110.0 %collective-permute-start.10 = (f32[512,128]{1,0:T(8,128)}, f32[512,128]{1,0:T(8,128)}, u32[]{:S(2)}, u32[]{:S(2)}) collective-permute-start(f32[512,128]{1,0:T(8,128)} %bitcast.27), channel_id=1, source_target_pairs={{0,1},{1,2},{2,3},{3,4},{4,5},{5,6},{6,7},{7,8},{8,9},{9,10},{10,1... | collective-permute-start | bytes 786440 | tf_op jit(solution)/shard_map/ppermute | solution.py:13
  250.9 3.1 copy-start
  256.9 1.2 copy-start.1
  264.3 3.1 copy-start
  270.2 1.2 copy-start.1
  277.6 3.1 copy-start
  283.5 1.2 copy-start.1
  290.9 3.1 copy-start
  296.8 1.2 copy-start.1
  304.2 3.1 copy-start
  310.2 1.2 copy-start.1
  317.5 3.1 copy-start
  323.5 1.2 copy-start.1
  324.7 20.2 %collective-permute-start.7 = (f32[512,128]{1,0:T(8,128)}, f32[512,128]{1,0:T(8,128)S(1)}, u32[]{:S(2)}, u32[]{:S(2)}) collective-permute-start(f32[512,128]{1,0:T(8,128)} %bitcast.127), channel_id=1, source_target_pairs={{16,0},{32,16},{48,32},{17,1},{33,17},{49,33},{18,2},{34,18},{50,3... | collective-permute-start | bytes 786440 | tf_op jit(solution)/shard_map/ppermute | solution.py:13
  328.9 22.1 %collective-permute-start.4 = (f32[512,128]{1,0:T(8,128)}, f32[512,128]{1,0:T(8,128)S(1)}, u32[]{:S(2)}, u32[]{:S(2)}) collective-permute-start(f32[512,128]{1,0:T(8,128)} %bitcast.126), channel_id=1, source_target_pairs={{16,0},{32,16},{48,32},{17,1},{33,17},{49,33},{18,2},{34,18},{50,3... | collective-permute-start | bytes 786440 | tf_op jit(solution)/shard_map/ppermute | solution.py:13
  333.2 3.0 copy-start.2
  336.2 17.6 %collective-permute-start.9 = (f32[512,128]{1,0:T(8,128)S(1)}, f32[512,128]{1,0:T(8,128)S(1)}, u32[]{:S(2)}, u32[]{:S(2)}) collective-permute-start(f32[512,128]{1,0:T(8,128)S(1)} %bitcast.125), channel_id=1, source_target_pairs={{1,0},{2,1},{3,2},{4,3},{5,4},{6,5},{7,6},{8,7},{9,8},{10,9},{11,1... | collective-permute-start | bytes 786440 | tf_op jit(solution)/shard_map/ppermute | solution.py:13
  337.5 25.6 %collective-permute-start.15 = (f32[512,128]{1,0:T(8,128)}, f32[512,128]{1,0:T(8,128)S(1)}, u32[]{:S(2)}, u32[]{:S(2)}) collective-permute-start(f32[512,128]{1,0:T(8,128)} %collective-permute-done.14), channel_id=1, source_target_pairs={{0,1},{1,2},{2,3},{3,4},{4,5},{5,6},{6,7},{7,8},{8,9},{9,10},{10,1... | collective-permute-start | bytes 786440 | tf_op jit(solution)/shard_map/ppermute | solution.py:13
  343.6 19.5 %collective-permute-start.12 = (f32[512,128]{1,0:T(8,128)}, f32[512,128]{1,0:T(8,128)S(1)}, u32[]{:S(2)}, u32[]{:S(2)}) collective-permute-start(f32[512,128]{1,0:T(8,128)} %collective-permute-done.11), channel_id=1, source_target_pairs={{1,0},{2,1},{3,2},{4,3},{5,4},{6,5},{7,6},{8,7},{9,8},{10,9},{11,1... | collective-permute-start | bytes 786440 | tf_op jit(solution)/shard_map/ppermute | solution.py:13
  344.9 23.9 %collective-permute-start.8 = (f32[512,128]{1,0:T(8,128)S(1)}, f32[512,128]{1,0:T(8,128)S(1)}, u32[]{:S(2)}, u32[]{:S(2)}) collective-permute-start(f32[512,128]{1,0:T(8,128)S(1)} %collective-permute-done.7), channel_id=1, source_target_pairs={{0,1},{1,2},{2,3},{3,4},{4,5},{5,6},{6,7},{7,8},{8,9},{9,10},{10,1... | collective-permute-start | bytes 786440 | tf_op jit(solution)/shard_map/ppermute | solution.py:13
  351.0 17.8 %collective-permute-start.5 = (f32[512,128]{1,0:T(8,128)S(1)}, f32[512,128]{1,0:T(8,128)S(1)}, u32[]{:S(2)}, u32[]{:S(2)}) collective-permute-start(f32[512,128]{1,0:T(8,128)S(1)} %collective-permute-done.4), channel_id=1, source_target_pairs={{1,0},{2,1},{3,2},{4,3},{5,4},{6,5},{7,6},{8,7},{9,8},{10,9},{11,1... | collective-permute-start | bytes 786440 | tf_op jit(solution)/shard_map/ppermute | solution.py:13
Sparse Core Ops, SparseCore 0:
  336.3 271.4 all-reduce.1
where the time goes:
time: 621 us; the launch traced here: 618 us
  waiting for transfers between devices  261 us (42%)
  other arithmetic  152 us (24%)
  local copies, waits for them, and re-layouts  81.9 us (13%)
  starting transfers between devices  49.9 us (8%)
  matrix products  49.6 us (8%)
  between operations  15 us (2%)
  loops' own time  7.98 us (1%)
    psum x1, waiting for transfers between devices, local(): weight_grad = lax.psum(scaled_part, ('dp', 'sx', 'sy'))  236 us
    scatter-add x6, other arithmetic, grad_group(): accum.at[picks.reshape(-1)]  137 us
    ppermute x12, starting transfers between devices, shifted(): return lax.ppermute(block, axis, route)  39.9 us
    transpose x6, local copies, waits for them, and re-layouts, grad_group(): jnp.einsum('gvd,kcd->kgvc', grad_rows, weights, preferred_element_type=jn...  20.1 us
    dot_general x6, matrix products, forward_group(): jnp.einsum('kgvc,kcd->gvd', gathered, weights, preferred_element_type=jnp...  18.2 us
    dot_general x6, matrix products, forward_group(): jnp.einsum('kgvc,gvd->kcd', gathered, grad_rows, preferred_element_type=j...  17.3 us
    gather x6, local copies, waits for them, and re-layouts, forward_group(): gathered = extended[picks]  16.4 us
    ppermute x12, waiting for transfers between devices, shifted(): return lax.ppermute(block, axis, route)  15 us
  transfers between devices with their start and end apart: 17, of which 4 were waited for; matrix products, arithmetic and copies ran while one was open for 44% of the time, Pallas kernels for 0%

commit v1 on v0

--- a/solution.py
+++ b/solution.py
@@ -106,7 +106,7 @@
         num_blocks * width_block * lax.axis_size("dp") * lax.axis_size("sx") * lax.axis_size("sy")
     )
     scaled_part = weight_part * (1.0 / math.sqrt(total))
-    weight_grad = lax.psum(scaled_part, ("dp", "sx", "sy"))
+    weight_grad = lax.psum(lax.psum(scaled_part, ("sx", "sy")), "dp")
     return (output, input_grad, weight_grad)
 
 

time: 621 us -> 576 us (0.928)
  waiting for transfers between devices: 261 us -> 223 us
    psum x1 -> x2, waiting for transfers between devices: 236 us -> 192 us  [local(): weight_grad = lax.psum(lax.psum(scaled_part, ('sx', 'sy')), 'dp')]
    ppermute x2, waiting for transfers between devices: 0.01 us -> 16.5 us  [padded(): lax.ppermute(tail, axis, [(i, (i + 1) % count) for i in range(ends)])]
    ppermute x2, waiting for transfers between devices: 9.99 us -> 0.08 us  [padded(): lax.ppermute(head, axis, [((i + 1) % count, i) for i in range(ends)])]
  transfers between devices with their start and end apart: 17 -> 18, of which waited for: 4 -> 7; matrix products, arithmetic and copies ran while one was open for 44% -> 33% of each run, Pallas kernels for 0% -> 0%
where the time goes in v1:
time: 576 us; the launch traced here: 571 us
  waiting for transfers between devices  223 us (39%)
  other arithmetic  151 us (26%)
  local copies, waits for them, and re-layouts  81 us (14%)
  matrix products  47.6 us (8%)
  starting transfers between devices  44.8 us (8%)
  between operations  15 us (3%)
  loops' own time  8.06 us (1%)
    psum x2, waiting for transfers between devices, local(): weight_grad = lax.psum(lax.psum(scaled_part, ('sx', 'sy')), 'dp')  192 us
    scatter-add x6, other arithmetic, grad_group(): accum.at[picks.reshape(-1)]  138 us
    ppermute x12, starting transfers between devices, shifted(): return lax.ppermute(block, axis, route)  35.4 us
    transpose x6, local copies, waits for them, and re-layouts, grad_group(): jnp.einsum('gvd,kcd->kgvc', grad_rows, weights, preferred_element_type=jn...  20.1 us
    dot_general x6, matrix products, forward_group(): jnp.einsum('kgvc,kcd->gvd', gathered, weights, preferred_element_type=jnp...  18.2 us
    dot_general x6, matrix products, forward_group(): jnp.einsum('kgvc,gvd->kcd', gathered, grad_rows, preferred_element_type=j...  17.4 us
    ppermute x2, waiting for transfers between devices, padded(): lax.ppermute(tail, axis, [(i, (i + 1) % count) for i in range(ends)])  16.5 us
    gather x6, local copies, waits for them, and re-layouts, forward_group(): gathered = extended[picks]  16.4 us
  transfers between devices with their start and end apart: 18, of which 7 were waited for; matrix products, arithmetic and copies ran while one was open for 33% of the time, Pallas kernels for 0%

profile of v1, /device:TPU:2, one launch (start us, length us, event | category | flops | bytes accessed | tf_op | source)
XLA Modules:
  0.0 570.6 jit_solution(6021334607917595484)
XLA Ops:
  8.5 3.2 constant_dynamic-update-slice_fusion.9
  14.3 2.4 collective-permute-start
  16.8 4.4 collective-permute-done
  21.2 3.7 collective-permute-start.2
  26.9 12.1 %collective-permute-done.2 = bf16[3,1,512,128]{3,2,1,0:T(8,128)(2,1)S(1)} collective-permute-done((bf16[3,1,512,128]{3,2,1,0:T(8,128)(2,1)S(1)}, bf16[3,1,512,128]{3,2,1,0:T(8,128)(2,1)S(1)}, u32[]{:S(2)}, u32[]{:S(2)}) %collective-permute-start.2) | collective-permute-done | bytes 393248 | tf_op jit(solution)/shard_map/ppermute | solution.py:24
  45.5 80.3 %while.24 = (s32[]{:T(128)}, f32[27,128,128]{2,1,0:T(8,128)}, bf16[6,4,128,128]{3,2,1,0:T(8,128)(2,1)}, s32[6]{0:T(128)}, s32[27,24]{1,0:T(8,128)}, /*index=5*/b...) while((s32[]{:T(128)}, f32[27,128,128]{2,1,0:T(8,128)}, ...), condition=%wide.region_1.0_spmd.clone, body=%wide.region_0.1_spmd.clone.sunk | while | flops 906986816 | bytes 33004880 | solution.py:101
  49.0 2.7 gather_fusion
  51.8 3.0 fusion.39
  54.8 2.9 bitcast_add_fusion.2
  62.4 2.7 gather_fusion
  65.2 3.0 fusion.39
  68.2 2.9 bitcast_add_fusion.2
  75.8 2.7 gather_fusion
  78.6 3.0 fusion.39
  81.6 2.9 bitcast_add_fusion.2
  89.2 2.7 gather_fusion
  91.9 3.0 fusion.39
  95.0 2.9 bitcast_add_fusion.2
  102.6 2.7 gather_fusion
  105.3 3.0 fusion.39
  108.4 2.9 bitcast_add_fusion.2
  116.0 2.7 gather_fusion
  118.7 3.0 fusion.39
  121.8 2.9 bitcast_add_fusion.2
  125.9 2.9 broadcast_multiply_fusion
  128.9 191.7 %all-reduce.3.cloned.1.call-done = f32[27,128,128]{2,1,0:T(8,128)} async-done(((f32[27,128,128]{2,1,0:T(8,128)}), f32[27,128,128]{2,1,0:T(8,128)}) %all-reduce.3.cloned.1.call-update) | async-done | bytes 1769488 | tf_op jit(solution)/shard_map/psum | solution.py:109
  323.1 182.7 %while.23 = (s32[]{:T(128)}, f32[57,128,128]{2,1,0:T(8,128)}, s32[6]{0:T(128)S(1)}, s32[27,24]{1,0:T(8,128)}, bf16[24,128,128]{2,1,0:T(8,128)(2,1)}, /*index=5*/...) while((s32[]{:T(128)}, f32[57,128,128]{2,1,0:T(8,128)}, s32[6]{0:T(128)S(1)}, ...), condition=%wide.region_4.5_spmd, body=%wide.region_2.0_spmd.sunk | while | flops 454754624 | bytes 43486336 | solution.py:61
  327.2 3.3 copy.22
  330.6 23.0 %scatter_fusion = f32[57,128,128]{2,1,0:T(8,128)} fusion(f32[57,128,128]{2,1,0:T(8,128)} %get-tuple-element.307, s32[108]{0:T(128)S(1)} %fusion.33, f32[108,128,128]{2,1,0:T(8,128)} %bitcast.107), kind=kCustom, calls=%fused_computation.2.clone.1 | custom fusion | flops 1769472 | bytes 21234096 | tf_op jit(solution)/shard_map/while/body/eval_jaxpr/scatter-add | solution.py:55
  357.7 3.3 copy.22
  361.1 23.1 %scatter_fusion = f32[57,128,128]{2,1,0:T(8,128)} fusion(f32[57,128,128]{2,1,0:T(8,128)} %get-tuple-element.307, s32[108]{0:T(128)S(1)} %fusion.33, f32[108,128,128]{2,1,0:T(8,128)} %bitcast.107), kind=kCustom, calls=%fused_computation.2.clone.1 | custom fusion | flops 1769472 | bytes 21234096 | tf_op jit(solution)/shard_map/while/body/eval_jaxpr/scatter-add | solution.py:55
  388.3 3.3 copy.22
  391.7 22.8 %scatter_fusion = f32[57,128,128]{2,1,0:T(8,128)} fusion(f32[57,128,128]{2,1,0:T(8,128)} %get-tuple-element.307, s32[108]{0:T(128)S(1)} %fusion.33, f32[108,128,128]{2,1,0:T(8,128)} %bitcast.107), kind=kCustom, calls=%fused_computation.2.clone.1 | custom fusion | flops 1769472 | bytes 21234096 | tf_op jit(solution)/shard_map/while/body/eval_jaxpr/scatter-add | solution.py:55
  418.6 3.3 copy.22
  422.0 23.0 %scatter_fusion = f32[57,128,128]{2,1,0:T(8,128)} fusion(f32[57,128,128]{2,1,0:T(8,128)} %get-tuple-element.307, s32[108]{0:T(128)S(1)} %fusion.33, f32[108,128,128]{2,1,0:T(8,128)} %bitcast.107), kind=kCustom, calls=%fused_computation.2.clone.1 | custom fusion | flops 1769472 | bytes 21234096 | tf_op jit(solution)/shard_map/while/body/eval_jaxpr/scatter-add | solution.py:55
  449.1 3.3 copy.22
  452.5 22.9 %scatter_fusion = f32[57,128,128]{2,1,0:T(8,128)} fusion(f32[57,128,128]{2,1,0:T(8,128)} %get-tuple-element.307, s32[108]{0:T(128)S(1)} %fusion.33, f32[108,128,128]{2,1,0:T(8,128)} %bitcast.107), kind=kCustom, calls=%fused_computation.2.clone.1 | custom fusion | flops 1769472 | bytes 21234096 | tf_op jit(solution)/shard_map/while/body/eval_jaxpr/scatter-add | solution.py:55
  479.5 3.3 copy.22
  482.8 22.9 %scatter_fusion = f32[57,128,128]{2,1,0:T(8,128)} fusion(f32[57,128,128]{2,1,0:T(8,128)} %get-tuple-element.307, s32[108]{0:T(128)S(1)} %fusion.33, f32[108,128,128]{2,1,0:T(8,128)} %bitcast.107), kind=kCustom, calls=%fused_computation.2.clone.1 | custom fusion | flops 1769472 | bytes 21234096 | tf_op jit(solution)/shard_map/while/body/eval_jaxpr/scatter-add | solution.py:55
  509.4 3.6 collective-permute-start.6
  516.9 3.4 collective-permute-start.10
  520.2 4.0 collective-permute-start.7
  524.2 2.7 collective-permute-start.4
  528.3 6.1 %collective-permute-start.15 = (f32[512,128]{1,0:T(8,128)S(1)}, f32[512,128]{1,0:T(8,128)S(1)}, u32[]{:S(2)}, u32[]{:S(2)}) collective-permute-start(f32[512,128]{1,0:T(8,128)S(1)} %collective-permute-done.14), channel_id=1, source_target_pairs={{0,1},{1,2},{2,3},{3,4},{4,5},{5,6},{6,7},{7,8},{8,9},{9,10},{10,1... | collective-permute-start | bytes 786440 | tf_op jit(solution)/shard_map/ppermute | solution.py:13
  535.7 6.1 %collective-permute-start.8 = (f32[512,128]{1,0:T(8,128)S(1)}, f32[512,128]{1,0:T(8,128)S(1)}, u32[]{:S(2)}, u32[]{:S(2)}) collective-permute-start(f32[512,128]{1,0:T(8,128)S(1)} %collective-permute-done.7), channel_id=1, source_target_pairs={{0,1},{1,2},{2,3},{3,4},{4,5},{5,6},{6,7},{7,8},{8,9},{9,10},{10,1... | collective-permute-start | bytes 786440 | tf_op jit(solution)/shard_map/ppermute | solution.py:13
  546.1 8.6 %collective-permute-done.15 = f32[512,128]{1,0:T(8,128)S(1)} collective-permute-done((f32[512,128]{1,0:T(8,128)S(1)}, f32[512,128]{1,0:T(8,128)S(1)}, u32[]{:S(2)}, u32[]{:S(2)}) %collective-permute-start.15) | collective-permute-done | bytes 262176 | tf_op jit(solution)/shard_map/ppermute | solution.py:13
  554.7 4.3 collective-permute-done.8
  560.9 2.9 copy.53
  (141 shorter events, 75.7 us)
Async XLA Ops:
  7.2 313.5 %all-reduce.3.cloned.1.call-start = ((), (), s32[]{:S(2)}) async-start(), calls=%async_computation | async-start | bytes 3538944 | tf_op jit(solution)/shard_map/psum | solution.py:109
  8.5 16.4 %copy-start.3 = (s32[1,1,1,27,24]{3,4,2,1,0:T(8,128)S(1)}, s32[1,1,1,27,24]{3,4,2,1,0:T(8,128)}, u32[]{:S(2)}) copy-start(s32[1,1,1,27,24]{3,4,2,1,0:T(8,128)} %param.13) | copy-start | bytes 7780
  12.3 4.4 collective-permute-start.1
  14.3 6.9 %collective-permute-start = (bf16[1,1,512,128]{3,2,1,0:T(8,128)(2,1)S(1)}, bf16[1,1,512,128]{3,2,1,0:T(8,128)(2,1)S(1)}, u32[]{:S(2)}, u32[]{:S(2)}) collective-permute-start(bf16[1,1,512,128]{3,2,1,0:T(8,128)(2,1)S(1)} %bitcast.120), channel_id=1, source_target_pairs={{0,16},{16,32},{32,48},{1,17},{17,33},{33,49},{2,18},{18,34},{34,5... | collective-permute-start | bytes 393224 | tf_op jit(solution)/shard_map/ppermute | solution.py:24
  21.2 17.8 %collective-permute-start.2 = (bf16[3,1,512,128]{3,2,1,0:T(8,128)(2,1)S(1)}, bf16[3,1,512,128]{3,2,1,0:T(8,128)(2,1)S(1)}, u32[]{:S(2)}, u32[]{:S(2)}) collective-permute-start(bf16[3,1,512,128]{3,2,1,0:T(8,128)(2,1)S(1)} %pad_maximum_fusion), channel_id=1, source_target_pairs={{0,1},{1,2},{2,3},{3,4},{4,5},{5,6},{6,7},{7,8},{8,9},{9,10},{10,1... | collective-permute-start | bytes 1179656 | tf_op jit(solution)/shard_map/ppermute | solution.py:24
  25.6 14.7 %collective-permute-start.3 = (bf16[3,1,512,128]{3,2,1,0:T(8,128)(2,1)S(1)}, bf16[3,1,512,128]{3,2,1,0:T(8,128)(2,1)S(1)}, u32[]{:S(2)}, u32[]{:S(2)}) collective-permute-start(bf16[3,1,512,128]{3,2,1,0:T(8,128)(2,1)S(1)} %pad_maximum_fusion), channel_id=1, source_target_pairs={{1,0},{2,1},{3,2},{4,3},{5,4},{6,5},{7,6},{8,7},{9,8},{10,9},{11,1... | collective-permute-start | bytes 1179656 | tf_op jit(solution)/shard_map/ppermute | solution.py:26
  51.8 3.1 copy-start
  57.7 1.2 copy-start.1
  65.2 3.1 copy-start
  71.1 1.2 copy-start.1
  78.5 3.1 copy-start
  84.5 1.2 copy-start.1
  91.9 3.1 copy-start
  97.9 1.2 copy-start.1
  105.3 3.1 copy-start
  111.3 1.2 copy-start.1
  118.7 3.1 copy-start
  124.7 1.2 copy-start.1
  128.8 432.1 %all-reduce.5.cloned.1.call-start = ((), (), s32[]{:S(2)}) async-start(), calls=%async_computation.1 | async-start | bytes 3538944 | tf_op jit(solution)/shard_map/psum | solution.py:109
  320.7 2.4 copy-start.2
  507.4 12.8 %collective-permute-start.14 = (f32[512,128]{1,0:T(8,128)S(1)}, f32[512,128]{1,0:T(8,128)S(1)}, u32[]{:S(2)}, u32[]{:S(2)}) collective-permute-start(f32[512,128]{1,0:T(8,128)S(1)} %bitcast.132), channel_id=1, source_target_pairs={{0,16},{16,32},{32,48},{1,17},{17,33},{33,49},{2,18},{18,34},{34,5... | collective-permute-start | bytes 786440 | tf_op jit(solution)/shard_map/ppermute | solution.py:13
  509.4 14.9 %collective-permute-start.6 = (f32[512,128]{1,0:T(8,128)S(1)}, f32[512,128]{1,0:T(8,128)S(1)}, u32[]{:S(2)}, u32[]{:S(2)}) collective-permute-start(f32[512,128]{1,0:T(8,128)S(1)} %bitcast.131), channel_id=1, source_target_pairs={{16,0},{32,16},{48,32},{17,1},{33,17},{49,33},{18,2},{34,18},{50,3... | collective-permute-start | bytes 786440 | tf_op jit(solution)/shard_map/ppermute | solution.py:13
  513.0 13.9 %collective-permute-start.13 = (f32[512,128]{1,0:T(8,128)S(1)}, f32[512,128]{1,0:T(8,128)S(1)}, u32[]{:S(2)}, u32[]{:S(2)}) collective-permute-start(f32[512,128]{1,0:T(8,128)S(1)} %bitcast.130), channel_id=1, source_target_pairs={{0,16},{16,32},{32,48},{1,17},{17,33},{33,49},{2,18},{18,34},{34,5... | collective-permute-start | bytes 786440 | tf_op jit(solution)/shard_map/ppermute | solution.py:13
  514.9 13.3 %collective-permute-start.11 = (f32[512,128]{1,0:T(8,128)S(1)}, f32[512,128]{1,0:T(8,128)S(1)}, u32[]{:S(2)}, u32[]{:S(2)}) collective-permute-start(f32[512,128]{1,0:T(8,128)S(1)} %bitcast.129), channel_id=1, source_target_pairs={{0,16},{16,32},{32,48},{1,17},{17,33},{33,49},{2,18},{18,34},{34,5... | collective-permute-start | bytes 786440 | tf_op jit(solution)/shard_map/ppermute | solution.py:13
  516.9 17.5 %collective-permute-start.10 = (f32[512,128]{1,0:T(8,128)S(1)}, f32[512,128]{1,0:T(8,128)S(1)}, u32[]{:S(2)}, u32[]{:S(2)}) collective-permute-start(f32[512,128]{1,0:T(8,128)S(1)} %bitcast.128), channel_id=1, source_target_pairs={{0,1},{1,2},{2,3},{3,4},{4,5},{5,6},{6,7},{7,8},{8,9},{9,10},{10,1... | collective-permute-start | bytes 786440 | tf_op jit(solution)/shard_map/ppermute | solution.py:13
  520.2 15.4 %collective-permute-start.7 = (f32[512,128]{1,0:T(8,128)S(1)}, f32[512,128]{1,0:T(8,128)S(1)}, u32[]{:S(2)}, u32[]{:S(2)}) collective-permute-start(f32[512,128]{1,0:T(8,128)S(1)} %bitcast.127), channel_id=1, source_target_pairs={{16,0},{32,16},{48,32},{17,1},{33,17},{49,33},{18,2},{34,18},{50,3... | collective-permute-start | bytes 786440 | tf_op jit(solution)/shard_map/ppermute | solution.py:13
  524.2 19.1 %collective-permute-start.4 = (f32[512,128]{1,0:T(8,128)S(1)}, f32[512,128]{1,0:T(8,128)S(1)}, u32[]{:S(2)}, u32[]{:S(2)}) collective-permute-start(f32[512,128]{1,0:T(8,128)S(1)} %bitcast.126), channel_id=1, source_target_pairs={{16,0},{32,16},{48,32},{17,1},{33,17},{49,33},{18,2},{34,18},{50,3... | collective-permute-start | bytes 786440 | tf_op jit(solution)/shard_map/ppermute | solution.py:13
  526.9 19.2 %collective-permute-start.9 = (f32[512,128]{1,0:T(8,128)S(1)}, f32[512,128]{1,0:T(8,128)S(1)}, u32[]{:S(2)}, u32[]{:S(2)}) collective-permute-start(f32[512,128]{1,0:T(8,128)S(1)} %bitcast.125), channel_id=1, source_target_pairs={{1,0},{2,1},{3,2},{4,3},{5,4},{6,5},{7,6},{8,7},{9,8},{10,9},{11,1... | collective-permute-start | bytes 786440 | tf_op jit(solution)/shard_map/ppermute | solution.py:13
  528.3 26.4 %collective-permute-start.15 = (f32[512,128]{1,0:T(8,128)S(1)}, f32[512,128]{1,0:T(8,128)S(1)}, u32[]{:S(2)}, u32[]{:S(2)}) collective-permute-start(f32[512,128]{1,0:T(8,128)S(1)} %collective-permute-done.14), channel_id=1, source_target_pairs={{0,1},{1,2},{2,3},{3,4},{4,5},{5,6},{6,7},{7,8},{8,9},{9,10},{10,1... | collective-permute-start | bytes 786440 | tf_op jit(solution)/shard_map/ppermute | solution.py:13
  534.3 20.3 %collective-permute-start.12 = (f32[512,128]{1,0:T(8,128)S(1)}, f32[512,128]{1,0:T(8,128)S(1)}, u32[]{:S(2)}, u32[]{:S(2)}) collective-permute-start(f32[512,128]{1,0:T(8,128)S(1)} %collective-permute-done.11), channel_id=1, source_target_pairs={{1,0},{2,1},{3,2},{4,3},{5,4},{6,5},{7,6},{8,7},{9,8},{10,9},{11,1... | collective-permute-start | bytes 786440 | tf_op jit(solution)/shard_map/ppermute | solution.py:13
  535.7 23.3 %collective-permute-start.8 = (f32[512,128]{1,0:T(8,128)S(1)}, f32[512,128]{1,0:T(8,128)S(1)}, u32[]{:S(2)}, u32[]{:S(2)}) collective-permute-start(f32[512,128]{1,0:T(8,128)S(1)} %collective-permute-done.7), channel_id=1, source_target_pairs={{0,1},{1,2},{2,3},{3,4},{4,5},{5,6},{6,7},{7,8},{8,9},{9,10},{10,1... | collective-permute-start | bytes 786440 | tf_op jit(solution)/shard_map/ppermute | solution.py:13
  543.3 15.7 %collective-permute-start.5 = (f32[512,128]{1,0:T(8,128)S(1)}, f32[512,128]{1,0:T(8,128)S(1)}, u32[]{:S(2)}, u32[]{:S(2)}) collective-permute-start(f32[512,128]{1,0:T(8,128)S(1)} %collective-permute-done.4), channel_id=1, source_target_pairs={{1,0},{2,1},{3,2},{4,3},{5,4},{6,5},{7,6},{8,7},{9,8},{10,9},{11,1... | collective-permute-start | bytes 786440 | tf_op jit(solution)/shard_map/ppermute | solution.py:13
Sparse Core Ops, SparseCore 0:
  128.9 191.6 all-reduce.2
  323.0 57.5 all-reduce.4
